TPU v7x, 32 devices: a whole 2x2x4 slice. The times are simulated.
32 devices in a mesh: loop: 4 (over y, x), bulk: 8 (over z, core).
Axes of the slice: x: 2, y: 2, z: 4, core: 2. Of those that a mesh axis runs over, the one named last changes fastest.
Arguments:
- series: float32 [4224, 3072], P('loop', 'bulk'), may hold values from -64 to 64
Outputs:
- correlation: float32 [4, 1056, 4224], P(None, 'bulk', 'loop')
All inputs are finite; a program needn't handle non-finite values.
Results may differ from a plain program's by a relative error of at most 0.0011.
Values may be sent and summed in bfloat16 or wider, within the bound.
A program may use at most 64 MiB of HBM per device.

v0:
```python
import jax
import jax.numpy as jnp
from jax import lax
from jax.sharding import PartitionSpec as P

TIME = 3072
epsilon = 1e-06


def normalize(centered, square_total):
    return (centered * lax.rsqrt(square_total / TIME + epsilon)).astype(jnp.bfloat16)


def contract(first_operand, second_operand):
    product = lax.dot_general(
        first_operand, second_operand, (((1,), (1,)), ((), ())), preferred_element_type=jnp.float32
    )
    return product / TIME


def cycle_gather(own_rows):
    return lax.all_gather(own_rows, "loop", axis=0, tiled=True)


def on_device(series):
    share_rows = series.shape[0] // lax.axis_size("bulk")
    average = lax.psum(jnp.sum(series, axis=1, keepdims=True), "bulk") / TIME
    centered = series - average
    squares = lax.psum(jnp.sum(centered * centered, axis=1, keepdims=True), "bulk")
    zscore = normalize(centered, squares)
    row_series = lax.all_gather(zscore, "bulk", axis=1, tiled=True)
    own_rows = lax.dynamic_slice_in_dim(
        row_series, lax.axis_index("bulk") * share_rows, share_rows, 0
    )
    gathered = contract(cycle_gather(own_rows), row_series)
    return gathered.reshape(lax.axis_size("loop"), share_rows, series.shape[0])


def solution(mesh):
    placed = (P("loop", "bulk"),)
    return jax.shard_map(
        on_device, mesh=mesh, in_specs=placed, out_specs=P(None, "bulk", "loop"), check_vma=False
    )
```

profile of v0, /device:TPU:0, one launch (start us, length us, event | category | flops | bytes accessed | tf_op | source)
XLA Modules:
  0.0 174.9 jit_solution(680406850263193112)
XLA Ops:
  6.5 0.0 copy-start
  6.5 0.0 all-gather.4.cloned.1.call-start
  6.5 1.8 %reduce_sum.18 = f32[1056]{0:T(1024)S(1)} reduce(f32[1056,384]{1,0:T(8,128)} %param.1, f32[]{:T(128)} %constant.7.clone.1), dimensions={1}, to_apply=%region_0.0 | reduce | flops 404448 | bytes 1626244 | tf_op jit(solution)/shard_map/reduce_sum | solution.py:27
  8.3 18.3 %psum.14 = f32[1056,1]{0,1:T(1,128)S(1)} all-reduce(f32[1056,1]{0,1:T(1,128)S(1)} %broadcast_in_dim.6), channel_id=1, replica_groups=mesh['loop'=4,'bulk'=8] {'bulk'}, use_global_device_ids=true, to_apply=%region_1.0 | all-reduce | flops 1056 | bytes 8448 | tf_op jit(solution)/shard_map/psum | solution.py:27
  26.7 0.0 copy-done
  26.7 0.4 multiply_reduce_fusion
  27.1 13.9 %psum.15 = f32[1056,1]{0,1:T(1,128)S(1)} all-reduce(f32[1056,1]{0,1:T(1,128)S(1)} %broadcast_in_dim.7), channel_id=1, replica_groups=mesh['loop'=4,'bulk'=8] {'bulk'}, use_global_device_ids=true, to_apply=%region_3.0 | all-reduce | flops 1056 | bytes 8448 | tf_op jit(solution)/shard_map/psum | solution.py:29
  41.1 1.2 multiply_convert_fusion
  42.3 0.0 all-gather.4.cloned.1.call-update
  42.3 0.0 all-gather.6.cloned.1.call-start
  42.4 64.4 %all-gather.4.cloned.1.call-done = bf16[1056,3072]{1,0:T(8,128)(2,1)} async-done(((bf16[1056,384]{1,0:T(8,128)(2,1)}), bf16[1056,3072]{1,0:T(8,128)(2,1)}) %all-gather.4.cloned.1.call-update) | async-done | bytes 6488080 | tf_op jit(solution)/shard_map/all_gather | solution.py:31
  106.8 2.3 %dynamic-slice_bitcast_fusion = bf16[1,132,3072]{2,1,0:T(8,128)(2,1)} fusion(bf16[1056,3072]{1,0:T(8,128)(2,1)} %all-gather.4.cloned.1.call-done, s32[]{:T(128)S(6)} %select_n.3), kind=kLoop, calls=%fused_computation.3 | loop fusion | bytes 1622020
  109.0 0.0 all-gather.6.cloned.1.call-update
  109.1 44.2 %all-gather.6.cloned.1.call-done = bf16[4,132,3072]{2,1,0:T(8,128)(2,1)} async-done(((bf16[1,132,3072]{2,1,0:T(8,128)(2,1)}), bf16[4,132,3072]{2,1,0:T(8,128)(2,1)}) %all-gather.6.cloned.1.call-update) | async-done | bytes 3244048 | tf_op jit(solution)/shard_map/all_gather | solution.py:22
  153.3 2.3 %reshape.5 = bf16[528,3072]{1,0:T(8,128)(2,1)S(1)} reshape(bf16[4,132,3072]{2,1,0:T(8,128)(2,1)} %all-gather.6.cloned.1.call-done) | data formatting | bytes 6488064
  155.6 8.7 %convolution_multiply_fusion = f32[528,1056]{1,0:T(8,128)} fusion(bf16[528,3072]{1,0:T(8,128)(2,1)S(1)} %reshape.5, bf16[1056,3072]{1,0:T(8,128)(2,1)} %all-gather.4.cloned.1.call-done), kind=kOutput, calls=%fused_computation | convolution fusion | flops 3426255360 | bytes 11962368 | tf_op jit(solution)/shard_map/dot_general | solution.py:15
  164.2 1.8 %reshape.3 = f32[4,132,1056]{2,1,0:T(8,128)S(1)} reshape(f32[528,1056]{1,0:T(8,128)} %convolution_multiply_fusion) | data formatting | bytes 4460544 | tf_op jit(solution)/shard_map/reshape | solution.py:36
  166.0 2.1 %copy.4 = f32[4,132,1056]{2,0,1:T(4,128)} copy(f32[4,132,1056]{2,1,0:T(8,128)S(1)} %reshape.3) | data formatting | bytes 4460544 | tf_op jit(solution)/shard_map/reshape | solution.py:36
  (4 shorter events, 0.1 us)
Async XLA Ops:
  6.5 20.2 %copy-start = (f32[1056,384]{1,0:T(8,128)S(1)}, f32[1056,384]{1,0:T(8,128)}, u32[]{:S(2)}) copy-start(f32[1056,384]{1,0:T(8,128)} %param.1) | copy-start | bytes 4866052
  6.5 100.2 %all-gather.4.cloned.1.call-start = ((), (), s32[]{:S(2)}) async-start(), calls=%async_computation | async-start | bytes 7299072 | tf_op jit(solution)/shard_map/all_gather | solution.py:31
  42.3 110.9 %all-gather.6.cloned.1.call-start = ((), (), s32[]{:S(2)}) async-start(), calls=%async_computation.1 | async-start | bytes 4177920 | tf_op jit(solution)/shard_map/all_gather | solution.py:22
Sparse Core Ops, SparseCore 0:
  42.5 64.2 all-gather.3
  109.2 44.0 all-gather.5
where the time goes:
time: 175 us
  waiting for transfers between devices  109 us (62%)
  blocking collectives  32.3 us (18%)
  between operations  13.5 us (8%)
  matrix products  8.65 us (5%)
  local copies, waits for them, and re-layouts  8.41 us (5%)
  other arithmetic  3.46 us (2%)
    all_gather x1, waiting for transfers between devices, on_device(): row_series = lax.all_gather(zscore, 'bulk', axis=1, tiled=True)  64.4 us
    all_gather x1, waiting for transfers between devices, cycle_gather(): return lax.all_gather(own_rows, 'loop', axis=0, tiled=True)  44.2 us
    psum x1, blocking collectives, on_device(): average = lax.psum(jnp.sum(series, axis=1, keepdims=True), 'bulk') / TIME  18.3 us
    psum x1, blocking collectives, on_device(): lax.psum(jnp.sum(centered * centered, axis=1, keepdims=True), 'bulk')  13.9 us
    dot_general x1, matrix products, contract(): lax.dot_general(first_operand, second_operand, (((1,), (1,)), ((), ())),...  8.65 us
    unnamed x4, local copies, waits for them, and re-layouts  4.55 us
    reshape x2, local copies, waits for them, and re-layouts, on_device(): return gathered.reshape(lax.axis_size('loop'), share_rows, series.shape[0])  3.84 us
  transfers between devices with their start and end apart: 2, of which 2 were waited for; matrix products, arithmetic and copies ran while one was open for 0% of the time, Pallas kernels for 0%

commit v1 on v0

--- a/solution.py
+++ b/solution.py
@@ -5,6 +5,11 @@
 
 TIME = 3072
 epsilon = 1e-06
+
+
+def all_by_exchange(shard, axis, along):
+    repeated = jnp.stack([shard] * lax.axis_size(axis))
+    return jnp.concatenate(lax.all_to_all(repeated, axis, 0, 0), axis=along)
 
 
 def normalize(centered, square_total):
@@ -19,7 +24,7 @@
 
 
 def cycle_gather(own_rows):
-    return lax.all_gather(own_rows, "loop", axis=0, tiled=True)
+    return all_by_exchange(own_rows, "loop", 0)
 
 
 def on_device(series):

time: 175 us -> 174 us (level)
  waiting for transfers between devices: 109 us -> 64.4 us
  blocking collectives: 32.3 us -> 75 us
    all_gather x1 -> x0, waiting for transfers between devices: 44.2 us -> none  [cycle_gather(): return lax.all_gather(own_rows, 'loop', axis=0, tiled=True)]
    all_to_all x0 -> x1, blocking collectives: none -> 42.7 us  [all_by_exchange(): return jnp.concatenate(lax.all_to_all(repeated, axis, 0, 0), axis=along)]
    unnamed x4 -> x2, local copies, waits for them, and re-layouts: 4.55 us -> 0.01 us
    reshape x0 -> x1, local copies, waits for them, and re-layouts: none -> 2.05 us  [all_by_exchange(): return jnp.concatenate(lax.all_to_all(repeated, axis, 0, 0), axis=along)]
  transfers between devices with their start and end apart: 2 -> 1, of which waited for: 2 -> 1; matrix products, arithmetic and copies ran while one was open for 0% -> 0% of each run, Pallas kernels for 0% -> 0%
where the time goes in v1:
time: 174 us
  blocking collectives  75 us (43%)
  waiting for transfers between devices  64.4 us (37%)
  between operations  13.5 us (8%)
  matrix products  9.65 us (6%)
  local copies, waits for them, and re-layouts  7.68 us (4%)
  other arithmetic  3.46 us (2%)
    all_gather x1, waiting for transfers between devices, on_device(): row_series = lax.all_gather(zscore, 'bulk', axis=1, tiled=True)  64.4 us
    all_to_all x1, blocking collectives, all_by_exchange(): return jnp.concatenate(lax.all_to_all(repeated, axis, 0, 0), axis=along)  42.7 us
    psum x1, blocking collectives, on_device(): average = lax.psum(jnp.sum(series, axis=1, keepdims=True), 'bulk') / TIME  18.3 us
    psum x1, blocking collectives, on_device(): lax.psum(jnp.sum(centered * centered, axis=1, keepdims=True), 'bulk')  13.9 us
    dot_general x1, matrix products, contract(): lax.dot_general(first_operand, second_operand, (((1,), (1,)), ((), ())),...  9.65 us
    reshape x2, local copies, waits for them, and re-layouts, on_device(): return gathered.reshape(lax.axis_size('loop'), share_rows, series.shape[0])  3.84 us
  transfers between devices with their start and end apart: 1, of which 1 were waited for; matrix products, arithmetic and copies ran while one was open for 0% of the time, Pallas kernels for 0%

profile of v1, /device:TPU:0, one launch (start us, length us, event | category | flops | bytes accessed | tf_op | source)
XLA Modules:
  0.0 173.7 jit_solution(8383527237116527347)
XLA Ops:
  6.5 0.0 copy-start
  6.5 0.0 all-gather.2.cloned.1.call-start
  6.5 1.8 %reduce_sum.18 = f32[1056]{0:T(1024)S(1)} reduce(f32[1056,384]{1,0:T(8,128)} %param.1, f32[]{:T(128)} %constant.7.clone.1), dimensions={1}, to_apply=%region_0.0 | reduce | flops 404448 | bytes 1626244 | tf_op jit(solution)/shard_map/reduce_sum | solution.py:32
  8.3 18.3 %psum.14 = f32[1056,1]{0,1:T(1,128)S(1)} all-reduce(f32[1056,1]{0,1:T(1,128)S(1)} %broadcast_in_dim.6), channel_id=1, replica_groups=mesh['loop'=4,'bulk'=8] {'bulk'}, use_global_device_ids=true, to_apply=%region_1.0 | all-reduce | flops 1056 | bytes 8448 | tf_op jit(solution)/shard_map/psum | solution.py:32
  26.7 0.0 copy-done
  26.7 0.4 multiply_reduce_fusion
  27.1 13.9 %psum.15 = f32[1056,1]{0,1:T(1,128)S(1)} all-reduce(f32[1056,1]{0,1:T(1,128)S(1)} %broadcast_in_dim.7), channel_id=1, replica_groups=mesh['loop'=4,'bulk'=8] {'bulk'}, use_global_device_ids=true, to_apply=%region_3.0 | all-reduce | flops 1056 | bytes 8448 | tf_op jit(solution)/shard_map/psum | solution.py:34
  41.1 1.2 multiply_convert_fusion
  42.3 0.0 all-gather.2.cloned.1.call-update
  42.3 64.4 %all-gather.2.cloned.1.call-done = bf16[1056,3072]{1,0:T(8,128)(2,1)} async-done(((bf16[1056,384]{1,0:T(8,128)(2,1)}), bf16[1056,3072]{1,0:T(8,128)(2,1)}) %all-gather.2.cloned.1.call-update) | async-done | bytes 6488080 | tf_op jit(solution)/shard_map/all_gather | solution.py:36
  106.8 1.4 constant_dynamic-slice_fusion
  108.1 0.4 stack.2
  108.6 42.7 %all_to_all.5 = bf16[4,132,3072]{2,1,0:T(8,128)(2,1)S(1)} all-to-all(bf16[4,132,3072]{2,1,0:T(8,128)(2,1)S(1)} %stack.2), channel_id=1, replica_groups=mesh['loop'=4,'bulk'=8] {'loop'}, dimensions={0} | all-to-all | bytes 6488064 | tf_op jit(solution)/shard_map/all_to_all | solution.py:12
  151.3 2.1 %reshape.8 = bf16[528,3072]{1,0:T(8,128)(2,1)} reshape(bf16[4,132,3072]{2,1,0:T(8,128)(2,1)S(1)} %all_to_all.5) | data formatting | bytes 6488064 | tf_op jit(solution)/shard_map/reshape | solution.py:12
  153.3 9.6 %convolution_multiply_fusion = f32[528,1056]{1,0:T(8,128)} fusion(bf16[528,3072]{1,0:T(8,128)(2,1)} %reshape.8, bf16[1056,3072]{1,0:T(8,128)(2,1)} %all-gather.2.cloned.1.call-done), kind=kOutput, calls=%fused_computation | convolution fusion | flops 3426255360 | bytes 11962368 | tf_op jit(solution)/shard_map/dot_general | solution.py:20
  163.0 1.8 %reshape.9 = f32[4,132,1056]{2,1,0:T(8,128)S(1)} reshape(f32[528,1056]{1,0:T(8,128)} %convolution_multiply_fusion) | data formatting | bytes 4460544 | tf_op jit(solution)/shard_map/reshape | solution.py:41
  164.8 2.1 %copy.3 = f32[4,132,1056]{2,0,1:T(4,128)} copy(f32[4,132,1056]{2,1,0:T(8,128)S(1)} %reshape.9) | data formatting | bytes 4460544 | tf_op jit(solution)/shard_map/reshape | solution.py:41
  (4 shorter events, 0.1 us)
Async XLA Ops:
  6.5 20.2 %copy-start = (f32[1056,384]{1,0:T(8,128)S(1)}, f32[1056,384]{1,0:T(8,128)}, u32[]{:S(2)}) copy-start(f32[1056,384]{1,0:T(8,128)} %param.1) | copy-start | bytes 4866052
  6.5 100.2 %all-gather.2.cloned.1.call-start = ((), (), s32[]{:S(2)}) async-start(), calls=%async_computation.1 | async-start | bytes 7299072 | tf_op jit(solution)/shard_map/all_gather | solution.py:36
Sparse Core Ops, SparseCore 0:
  42.5 64.2 all-gather.1
